TPU v7x, 32 devices: a whole 2x2x4 slice. The times are simulated.
32 devices in a mesh: runs: 1, cfg: 32 (over z, y, x, core).
Axes of the slice: x: 2, y: 2, z: 4, core: 2. Of those that a mesh axis runs over, the one named last changes fastest.
Arguments:
- amplitudes: float32 [2, 512, 128, 512], P('runs', 'cfg')
- prop_third: float32 [2, 512, 512], replicated
- bitmasks_first: int32 [512], replicated, may hold values from 0 to 10922, as said below
- bitmasks_second: int32 [128], replicated, may hold values from 0 to 10922, as said below
- bitmasks_third: int32 [512], P('cfg'), may hold values from 0 to 10922, as said below
- detune_steps: int32 [3], P('runs'), may hold values from 0 to 15
Outputs:
- density: float32 [512, 2, 512], P(('runs', 'cfg'))
Inputs may be any that keep to these rules, and one draw needn't show every extreme that they name: `bitmasks_first`: 512 different numbers, none with two adjacent bits set. `bitmasks_second`: 128 different numbers, none with two adjacent bits set. `bitmasks_third`: 512 different numbers, none with two adjacent bits set.
All inputs are finite; a program needn't handle non-finite values.
Results may differ from a plain program's by a relative error of at most 0.00005.
Values sent between devices are 32-bit elements; how exact they have to be, the bound alone decides.
A program may use at most 64 MiB of HBM per device.

v0:
```python
import jax
import jax.numpy as jnp
from jax import lax
from jax.sharding import PartitionSpec as P

angle_step = 0.2
pair_angle = 0.7
atom_count = 14


def atom_bit(bitmasks, which):
    return (jnp.right_shift(bitmasks, which) & 1).astype(jnp.float32)


def occupation(bitmasks):
    total = jnp.zeros(bitmasks.shape, jnp.float32)
    for which in range(atom_count):
        total = total + atom_bit(bitmasks, which)
    return total


def boundary_terms(first, second, third, detune_steps):
    scaled = detune_steps.astype(jnp.float32) * angle_step
    phase_first = scaled[0] * occupation(first)
    phase_second = scaled[1] * occupation(second)
    phase_third = scaled[2] * occupation(third)
    last_first = atom_bit(first, 13)[None, None, :]
    near_first = atom_bit(first, 12)[None, None, :]
    head_second = atom_bit(second, 0)[None, :, None]
    next_second = atom_bit(second, 1)[None, :, None]
    last_second = atom_bit(second, 13)[None, :, None]
    near_second = atom_bit(second, 12)[None, :, None]
    head_third = atom_bit(third, 0)[:, None, None]
    next_third = atom_bit(third, 1)[:, None, None]
    allowed = (1.0 - last_first * head_second) * (1.0 - last_second * head_third)
    pairs = (
        near_first * head_second
        + last_first * next_second
        + near_second * head_third
        + last_second * next_third
    )
    angle = (
        phase_third[:, None, None]
        + phase_second[None, :, None]
        + phase_first[None, None, :]
        + pair_angle * pairs
    )
    return (allowed, angle)


def apply_third(block, prop):

    def product(values, matrix):
        return jnp.einsum("ij,jba->iba", matrix, values, precision=lax.Precision.HIGHEST)

    real_part = product(block[0], prop[0]) - product(block[1], prop[1])
    imag_part = product(block[0], prop[1]) + product(block[1], prop[0])
    return jnp.stack([real_part, imag_part])


def inner_rows(left, right):
    return lax.dot_general(
        left,
        right,
        (((0,), (0,)), ((), ())),
        precision=lax.Precision.HIGHEST,
        preferred_element_type=jnp.float32,
    )


def shards(amplitudes, prop_third, bitmasks_first, bitmasks_second, bitmasks_third, detune_steps):
    allowed, angle = boundary_terms(bitmasks_first, bitmasks_second, bitmasks_third, detune_steps)
    cosine = jnp.cos(angle)
    sine = jnp.sin(angle)
    phased = jnp.stack(
        [
            allowed * (amplitudes[0] * cosine + amplitudes[1] * sine),
            allowed * (amplitudes[1] * cosine - amplitudes[0] * sine),
        ]
    )
    evolved = apply_third(
        lax.all_to_all(phased, "cfg", split_axis=2, concat_axis=1, tiled=True), prop_third
    )
    width = evolved.shape[3]
    flat_real = evolved[0].reshape(-1, width)
    flat_imag = evolved[1].reshape(-1, width)
    stacked = jnp.concatenate([flat_real, flat_imag], axis=0)
    local_real = inner_rows(stacked, stacked)
    crossed = inner_rows(flat_imag, flat_real)
    local_term = jnp.stack([local_real, crossed - crossed.T], axis=1)
    return lax.psum_scatter(local_term, "cfg", scatter_dimension=0, tiled=True)


def solution(mesh):
    placed = (P("runs", "cfg", None, None), P(), P(), P(), P("cfg"), P("runs"))
    return jax.shard_map(
        shards,
        mesh=mesh,
        in_specs=placed,
        out_specs=P(("runs", "cfg"), None, None),
        check_vma=False,
    )
```

profile of v0, /device:TPU:0, one launch (start us, length us, event | category | flops | bytes accessed | tf_op | source)
XLA Modules:
  0.0 469.0 jit_solution(2630011389610892652)
XLA Ops:
  6.5 0.0 reduce-scatter.2.cloned.1.call-start
  6.5 0.7 convert_multiply_fusion
  7.2 0.7 fusion.23
  7.8 0.7 and_convert_fusion.5
  8.5 1.3 add_multiply_fusion.2
  9.8 0.7 and_convert_fusion.7
  10.5 1.3 add_multiply_fusion.1
  11.8 0.7 and_convert_fusion.1
  12.5 1.3 add_multiply_fusion
  13.8 0.1 multiply_subtract_fusion.1
  13.9 0.1 copy.25
  14.0 0.1 copy.28
  14.1 0.1 copy.27
  14.2 4.5 fusion.22
  18.6 0.1 broadcast_add_fusion
  18.7 0.1 multiply_subtract_fusion
  18.9 18.9 %multiply_multiply_fusion.1 = (f32[1,16,128,512]{3,1,0,2:T(8,128)S(1)}, f32[1,16,128,512]{3,1,0,2:T(8,128)S(1)}) fusion(f32[1,16,128,512]{3,2,1,0:T(8,128)S(1)} %get-tuple-element.10, f32[1,16,128,512]{3,2,1,0:T(8,128)S(1)} %get-tuple-element.9, f32[16,128]{0,1:T(8,128)S(1)} %copy.28, f32[16,128]{0,1:T(8,128)S(1)} %copy.27, ...), kind=kLoop, calls=%fused_computation.7 | loop fusion | flops 14680064 | bytes 17336320 | tf_op jit(solution)/shard_map/mul | solution.py:77
  37.8 1.9 pad_maximum_fusion
  39.7 190.7 %all_to_all.15 = f32[2,16,128,512]{3,1,0,2:T(8,128)} all-to-all(f32[2,16,128,512]{3,1,0,2:T(8,128)S(1)} %pad_maximum_fusion), channel_id=1, replica_groups=mesh['runs'=1,'cfg'=32] {'cfg'}, dimensions={2} | all-to-all | bytes 16777216 | tf_op jit(solution)/shard_map/all_to_all | solution.py:82
  230.4 4.4 copy.44
  234.9 0.0 copy-start
  234.9 1.9 fusion.21
  236.8 0.0 copy-done
  236.8 8.0 %fusion.10 = f32[4,512,512]{1,2,0:T(8,128)S(1)} fusion(f32[512,4,512]{2,0,1:T(8,128)S(1)} %bitcast.43, f32[2,512,512]{2,1,0:T(8,128)S(1)} %copy-done), kind=kOutput, calls=%fused_computation.18 | convolution fusion | flops 6442450944 | bytes 9437184 | tf_op jit(solution)/shard_map/ij,jba->iba/dot_general | solution.py:54
  244.8 8.6 %fusion.14 = f32[4,512,512]{1,2,0:T(8,128)S(1)} fusion(f32[512,4,512]{2,0,1:T(8,128)S(1)} %bitcast.44, f32[2,512,512]{2,1,0:T(8,128)S(1)} %copy-done), kind=kOutput, calls=%fused_computation.22 | convolution fusion | flops 6442450944 | bytes 9437184 | tf_op jit(solution)/shard_map/ij,jba->iba/dot_general | solution.py:54
  253.5 9.1 %add_bitcast_fusion = f32[512,4,512]{2,0,1:T(8,128)S(1)} fusion(f32[4,512,512]{1,2,0:T(8,128)S(1)} %fusion.10, f32[512,4,512]{2,0,1:T(8,128)S(1)} %bitcast.41, f32[2,512,512]{2,1,0:T(8,128)S(1)} %copy-done), kind=kOutput, calls=%fused_computation.8 | convolution fusion | flops 6443499520 | bytes 13631488 | tf_op jit(solution)/shard_map/ij,jba->iba/dot_general | solution.py:54
  262.6 8.9 %subtract_bitcast_fusion = f32[512,4,512]{2,0,1:T(8,128)S(1)} fusion(f32[4,512,512]{1,2,0:T(8,128)S(1)} %fusion.14, f32[512,4,512]{2,0,1:T(8,128)S(1)} %bitcast.42, f32[2,512,512]{2,1,0:T(8,128)S(1)} %copy-done), kind=kOutput, calls=%fused_computation.9 | convolution fusion | flops 6443499520 | bytes 13631488 | tf_op jit(solution)/shard_map/ij,jba->iba/dot_general | solution.py:54
  271.5 4.7 copy.31
  276.2 7.5 %convolution_bitcast_fusion = f32[512,512]{1,0:T(8,128)S(1)} fusion(f32[512,4,512]{2,0,1:T(8,128)S(1)} %add_bitcast_fusion, f32[512,4,512]{2,0,1:T(8,128)S(1)} %subtract_bitcast_fusion), kind=kOutput, calls=%fused_computation.15 | convolution fusion | flops 6442450944 | bytes 9437184 | tf_op jit(solution)/shard_map/dot_general | solution.py:62
  283.7 4.6 copy.32
  288.3 5.3 %reshape_squeeze_stack.6 = f32[2048,512]{1,0:T(8,128)} reshape(f32[512,4,512]{2,1,0:T(4,128)} %copy.31) | data formatting | bytes 8388608 | tf_op jit(solution)/shard_map/reshape;squeeze;stack | solution.py:85
  293.6 5.3 %reshape_squeeze_stack.7 = f32[2048,512]{1,0:T(8,128)} reshape(f32[512,4,512]{2,1,0:T(4,128)} %copy.32) | data formatting | bytes 8388608 | tf_op jit(solution)/shard_map/reshape;squeeze;stack | solution.py:86
  299.0 0.3 copy.34
  299.3 0.2 fusion.9
  299.5 21.7 %fusion.6 = f32[512,1,512]{2,0,1:T(8,128)S(1)} fusion(f32[2048,512]{1,0:T(8,128)} %reshape_squeeze_stack.7, f32[2048,512]{1,0:T(8,128)} %reshape_squeeze_stack.6), kind=kOutput, calls=%fused_computation.14 | convolution fusion | flops 12886999040 | bytes 9437184 | tf_op jit(solution)/shard_map/dot_general | solution.py:62
  321.2 1.5 pad_maximum_fusion.1
  322.7 0.0 reduce-scatter.2.cloned.1.call-update
  322.8 137.7 %reduce-scatter.2.cloned.1.call-done = f32[16,2,512]{2,0,1:T(8,128)} async-done(((f32[512,2,512]{2,0,1:T(8,128)}), f32[16,2,512]{2,0,1:T(8,128)}) %reduce-scatter.2.cloned.1.call-update) | async-done | bytes 65552 | tf_op jit(solution)/shard_map/reduce_scatter | solution.py:91
  460.5 1.5 copy.35
Async XLA Ops:
  6.5 454.0 %reduce-scatter.2.cloned.1.call-start = ((), (), s32[]{:S(2)}) async-start(), calls=%async_computation.2 | async-start | bytes 2162688 | tf_op jit(solution)/shard_map/reduce_scatter | solution.py:91
  234.9 1.9 copy-start
Sparse Core Ops, SparseCore 0:
  322.9 137.5 reduce-scatter.1
where the time goes:
time: 478 us; the launch traced here: 469 us
  blocking collectives  191 us (40%)
  waiting for transfers between devices  138 us (29%)
  matrix products  63.8 us (13%)
  local copies, waits for them, and re-layouts  33.6 us (7%)
  other arithmetic  29.4 us (6%)
  between operations  13.7 us (3%)
    all_to_all x1, blocking collectives, shards(): lax.all_to_all(phased, 'cfg', split_axis=2, concat_axis=1, tiled=True)  191 us
    reduce_scatter x1, waiting for transfers between devices, shards(): return lax.psum_scatter(local_term, 'cfg', scatter_dimension=0, tiled=True)  138 us
    dot_general x4, matrix products, product(): jnp.einsum('ij,jba->iba', matrix, values, precision=lax.Precision.HIGHEST)  34.7 us
    dot_general x2, matrix products, inner_rows(): lax.dot_general(left, right, (((0,), (0,)), ((), ())), precision=lax.Prec...  29.2 us
    mul x1, other arithmetic, shards(): allowed * (amplitudes[0] * cosine + amplitudes[1] * sine)  18.9 us
  transfers between devices with their start and end apart: 1, of which 1 were waited for; matrix products, arithmetic and copies ran while one was open for 0% of the time, Pallas kernels for 0%

commit v1 on v0

v1 whole, which is shorter than its diff:
```python
import functools
import jax
import jax.numpy as jnp
from jax import lax
from jax.experimental import pallas as pl
from jax.experimental.pallas import tpu as pltpu
from jax.sharding import PartitionSpec as P

angle_step = 0.2
pair_angle = 0.7
atom_count = 14
MESH = pl.DeviceIdType.MESH


def atom_bit(bitmasks, which):
    return (jnp.right_shift(bitmasks, which) & 1).astype(jnp.float32)


def occupation(bitmasks):
    total = jnp.zeros(bitmasks.shape, jnp.float32)
    for which in range(atom_count):
        total = total + atom_bit(bitmasks, which)
    return total


def factor_tables(first, second, third, detune_steps):
    scaled = detune_steps.astype(jnp.float32) * angle_step
    phase_first = scaled[0] * occupation(first)
    phase_second = scaled[1] * occupation(second)
    phase_third = scaled[2] * occupation(third)
    head, following = atom_bit(second, 0)[:, None], atom_bit(second, 1)[:, None]
    near, last = atom_bit(second, 12)[None, :], atom_bit(second, 13)[None, :]
    angle_ba = (
        phase_second[:, None]
        + phase_first[None, :]
        + pair_angle * (atom_bit(first, 12)[None, :] * head + atom_bit(first, 13)[None, :] * following)
    )
    allowed_ba = 1.0 - atom_bit(first, 13)[None, :] * head
    angle_cb = phase_third[:, None] + pair_angle * (
        near * atom_bit(third, 0)[:, None] + last * atom_bit(third, 1)[:, None]
    )
    allowed_cb = 1.0 - last * atom_bit(third, 0)[:, None]
    return lax.optimization_barrier(
        (
            allowed_ba * jnp.cos(angle_ba),
            allowed_ba * jnp.sin(angle_ba),
            allowed_cb * jnp.cos(angle_cb),
            allowed_cb * jnp.sin(angle_cb),
        )
    )


def apply_phases(amplitudes, tables):
    cos_ba, sin_ba, cos_cb, sin_cb = tables
    cos_cb, sin_cb = cos_cb[:, :, None], sin_cb[:, :, None]
    cosine = cos_ba[None] * cos_cb - sin_ba[None] * sin_cb
    sine = sin_ba[None] * cos_cb + cos_ba[None] * sin_cb
    return jnp.stack(
        [
            amplitudes[0] * cosine + amplitudes[1] * sine,
            amplitudes[1] * cosine - amplitudes[0] * sine,
        ]
    )


def split(values):
    high = values.astype(jnp.bfloat16)
    return high, (values - high.astype(jnp.float32)).astype(jnp.bfloat16)


def dot3(left, right, dims):
    def one(a, b):
        return lax.dot_general(a, b, (dims, ((), ())), preferred_element_type=jnp.float32)

    return one(left[0], right[0]) + (one(left[0], right[1]) + one(left[1], right[0]))


def density_kernel(
    n, x_ref, ah_ref, al_ref, out_ref,
    recv, xh, xl, vh, vl, total, kept, landing,
    send_sem, recv_sem, half_send, half_recv,
):
    steps = half_send.shape[0]
    me = lax.axis_index("cfg")
    each_b, rows_c = x_ref.shape[1], x_ref.shape[3]
    width = x_ref.shape[4]
    height = recv.shape[2]
    rows = out_ref.shape[1]

    barrier = pltpu.get_barrier_semaphore()

    def greet(s, carry):
        pl.semaphore_signal(
            barrier, inc=1, device_id={"cfg": lax.rem(me + s, n)}, device_id_type=MESH
        )
        return carry

    lax.fori_loop(1, n, greet, 0)
    pl.semaphore_wait(barrier, n - 1)

    def place(b):
        return recv.at[b, :, pl.ds(pl.multiple_of(me * rows_c, rows_c), rows_c), :]

    def send(b, s):
        peer = lax.rem(me + s, n)
        pltpu.make_async_remote_copy(
            src_ref=x_ref.at[peer, b],
            dst_ref=place(b),
            send_sem=send_sem.at[b],
            recv_sem=recv_sem.at[b],
            device_id={"cfg": peer},
            device_id_type=MESH,
        ).start()

    def send_all(b, carry):
        pltpu.make_async_copy(x_ref.at[me, b], place(b), recv_sem.at[b]).start()

        def pair(s, inner):
            send(b, n // 2 + s)
            send(b, n // 2 - s)
            return inner

        send(b, n // 2)
        lax.fori_loop(1, n // 2, pair, 0)
        return carry

    lax.fori_loop(0, each_b, send_all, 0)
    total[...] = jnp.zeros_like(total)

    tile = 256
    pairs_per_tile = tile // (2 * rows)

    def work(b, carry):
        pltpu.make_async_copy(recv.at[b], recv.at[b], recv_sem.at[b]).wait()

        for part in range(2):
            def split_rows(t, inner):
                at = pl.ds(pl.multiple_of(t * 64, 64), 64)
                to = pl.ds(pl.multiple_of(part * height + t * 64, 64), 64)
                high, low = split(recv[b, part, at, :])
                xh[to, :] = high
                xl[to, :] = low
                return inner

            lax.fori_loop(0, height // 64, split_rows, 0)

        def evolve(t, inner):
            at = pl.ds(pl.multiple_of(t * tile, tile), tile)
            value = dot3(
                (ah_ref[at, :], al_ref[at, :]), (xh[...], xl[...]), ((1,), (0,))
            )
            high, low = split(value)
            vh[at, :] = high
            vl[at, :] = low
            return inner

        lax.fori_loop(0, 2 * height // tile, evolve, 0)

        for t in range(width // tile):
            at = slice(t * tile, (t + 1) * tile)
            real = (vh[:height, :], vl[:height, :])
            imag = (vh[height:, :], vl[height:, :])
            real_t = (vh[:height, at], vl[:height, at])
            imag_t = (vh[height:, at], vl[height:, at])
            dims = ((0,), (0,))
            term_real = dot3(real_t, real, dims) + dot3(imag_t, imag, dims)
            to = slice(t * pairs_per_tile, (t + 1) * pairs_per_tile)
            shape = (pairs_per_tile, 2, rows, width)
            total[0, to] += term_real.reshape(shape)
            term_imag = dot3(imag_t, real, dims) - dot3(real_t, imag, dims)
            total[1, to] += term_imag.reshape(shape)
        return carry

    lax.fori_loop(0, each_b, work, 0)

    def halve(step, src, half):
        other = me + (1 - 2 * lax.rem(me // (2 ** step), 2)) * (2 ** step)
        copy = pltpu.make_async_remote_copy(
            src_ref=src,
            dst_ref=landing.at[:, pl.ds(n - 2 * half, half)],
            send_sem=half_send.at[step],
            recv_sem=half_recv.at[step],
            device_id={"cfg": other},
            device_id_type=MESH,
        )
        copy.start()
        return copy

    half = n // 2
    bit = lax.rem(me, 2)
    copy = halve(0, total.at[:, :, 1 - bit], half)
    copy.wait()

    def add_first(i, carry):
        where = 0
        rest = i
        for _ in range(steps - 1):
            where = where * 2 + lax.rem(rest, 2)
            rest = rest // 2
        kept[:, where] = total[:, i, bit] + landing[:, i]
        return carry

    lax.fori_loop(0, half, add_first, 0)
    offset = 0
    for step in range(1, steps):
        half = half // 2
        bit = lax.rem(me // (2 ** step), 2)
        copy = halve(step, kept.at[:, pl.ds(offset + (1 - bit) * half, half)], half)
        offset = offset + bit * half
        copy.wait()

        def add_next(i, carry, offset=offset, half=half):
            kept[:, offset + i] += landing[:, n - 2 * half + i]
            return carry

        lax.fori_loop(0, half, add_next, 0)
    out_ref[...] = kept[:, offset]

    for b in range(each_b):
        pltpu.make_async_copy(
            x_ref.at[pl.ds(0, n - 1), b], x_ref.at[pl.ds(0, n - 1), b], send_sem.at[b]
        ).wait()


def fused_density(phased, prop, n):
    _, rows_c, total_b, width = phased.shape
    height = prop.shape[1]
    each_b = total_b // n
    rows = width // n
    steps = n.bit_length() - 1
    outgoing = jnp.transpose(phased, (2, 0, 1, 3)).reshape(n, each_b, 2, rows_c, width)
    joined = jnp.concatenate(
        [
            jnp.concatenate([prop[0], -prop[1]], axis=1),
            jnp.concatenate([prop[1], prop[0]], axis=1),
        ],
        axis=0,
    )
    high = lax.reduce_precision(joined, 8, 7)
    low = (joined - high).astype(jnp.bfloat16)
    high = high.astype(jnp.bfloat16)
    vmem = pl.BlockSpec(memory_space=pltpu.VMEM)
    result = pl.pallas_call(
        functools.partial(density_kernel, n),
        out_shape=jax.ShapeDtypeStruct((2, rows, width), jnp.float32),
        in_specs=[pl.BlockSpec(memory_space=pl.ANY), vmem, vmem],
        out_specs=vmem,
        scratch_shapes=[
            pltpu.VMEM((each_b, 2, height, width), jnp.float32),
            pltpu.VMEM((2 * height, width), jnp.bfloat16),
            pltpu.VMEM((2 * height, width), jnp.bfloat16),
            pltpu.VMEM((2 * height, width), jnp.bfloat16),
            pltpu.VMEM((2 * height, width), jnp.bfloat16),
            pltpu.VMEM((2, n // 2, 2, rows, width), jnp.float32),
            pltpu.VMEM((2, n // 2, rows, width), jnp.float32),
            pltpu.VMEM((2, n - 1, rows, width), jnp.float32),
            pltpu.SemaphoreType.DMA((each_b,)),
            pltpu.SemaphoreType.DMA((each_b,)),
            pltpu.SemaphoreType.DMA((steps,)),
            pltpu.SemaphoreType.DMA((steps,)),
        ],
        compiler_params=pltpu.CompilerParams(
            collective_id=0, has_side_effects=True, vmem_limit_bytes=50 * 2**20
        ),
    )(outgoing, high, low)
    return jnp.transpose(result, (1, 0, 2))


def plain_density(phased, prop):
    def product(values, matrix):
        return jnp.einsum("ij,jba->iba", matrix, values, precision=lax.Precision.HIGHEST)

    def inner_rows(left, right):
        return lax.dot_general(
            left,
            right,
            (((0,), (0,)), ((), ())),
            precision=lax.Precision.HIGHEST,
            preferred_element_type=jnp.float32,
        )

    block = lax.all_to_all(phased, "cfg", split_axis=2, concat_axis=1, tiled=True)
    width = block.shape[3]
    real = (product(block[0], prop[0]) - product(block[1], prop[1])).reshape(-1, width)
    imag = (product(block[0], prop[1]) + product(block[1], prop[0])).reshape(-1, width)
    stacked = jnp.concatenate([real, imag], axis=0)
    crossed = inner_rows(imag, real)
    term = jnp.stack([inner_rows(stacked, stacked), crossed - crossed.T], axis=1)
    return lax.psum_scatter(term, "cfg", scatter_dimension=0, tiled=True)


def shards(n, amplitudes, prop_third, first, second, third, detune_steps):
    phased = apply_phases(amplitudes, factor_tables(first, second, third, detune_steps))
    _, rows_c, total_b, width = phased.shape
    height = prop_third.shape[1]
    fits = (
        n > 1
        and n & (n - 1) == 0
        and total_b % n == 0
        and rows_c % 8 == 0
        and width % (8 * n) == 0
        and width % 256 == 0
        and height % 256 == 0
        and 256 % (2 * (width // n)) == 0
        and 4 * total_b // n * height * width * 2 <= 2**24
    )
    if fits:
        return fused_density(phased, prop_third, n)
    return plain_density(phased, prop_third)


def solution(mesh):
    placed = (P("runs", "cfg", None, None), P(), P(), P(), P("cfg"), P("runs"))
    return jax.shard_map(
        functools.partial(shards, mesh.shape["cfg"]),
        mesh=mesh,
        in_specs=placed,
        out_specs=P(("runs", "cfg"), None, None),
        check_vma=False,
    )
```

time: 478 us -> 258 us (0.54); the launches traced: 469 us -> 258 us
  Pallas kernels: 0 us -> 232 us
  blocking collectives: 191 us -> 0 us
  waiting for transfers between devices: 138 us -> 0 us
  matrix products: 63.8 us -> 0 us
  local copies, waits for them, and re-layouts: 33.6 us -> 9.55 us
  between operations: 13.7 us -> 0.06 us
  other arithmetic: 29.4 us -> 16.2 us
    pallas_call x0 -> x1, Pallas kernels: none -> 232 us  [fused_density(): pl.pallas_call(functools.partial(density_kernel, n), out_shape=jax.ShapeD...]
    all_to_all x1 -> x0, blocking collectives: 191 us -> none  [shards(): lax.all_to_all(phased, 'cfg', split_axis=2, concat_axis=1, tiled=True)]
    reduce_scatter x1 -> x0, waiting for transfers between devices: 138 us -> none  [shards(): return lax.psum_scatter(local_term, 'cfg', scatter_dimension=0, tiled=True)]
    dot_general x6 -> x0, matrix products: 63.8 us -> none  [the longest x4 34.7 us: product(): jnp.einsum('ij,jba->iba', matrix, values, precision=lax.Precision.HIGHEST)]
    mul x5 -> x6, other arithmetic: 23.5 us -> 5.83 us  [the longest x1 1.33 us: factor_tables(): phase_first = scaled[0] * occupation(first)]
    another operation x2 -> x0, local copies, waits for them, and re-layouts: 10.6 us -> none  [the longest x1 5.32 us: shards(): flat_imag = evolved[1].reshape(-1, width)]
    transpose x0 -> x2, local copies, waits for them, and re-layouts: none -> 8.76 us  [the longest x1 8.08 us: fused_density(): jnp.transpose(phased, (2, 0, 1, 3)).reshape(n, each_b, 2, rows_c, width)]
    slice x3 -> x1, local copies, waits for them, and re-layouts: 7.02 us -> 0.61 us  [factor_tables(): phase_third = scaled[2] * occupation(third)]
  transfers between devices with their start and end apart: 1 -> 0, of which waited for: 1 -> 0; matrix products, arithmetic and copies ran while one was open for 0% -> 0% of each run, Pallas kernels for 0% -> 0%
where the time goes in v1:
time: 258 us
  Pallas kernels  232 us (90%)
  other arithmetic  16.2 us (6%)
  local copies, waits for them, and re-layouts  9.55 us (4%)
    pallas_call x1, Pallas kernels, fused_density(): pl.pallas_call(functools.partial(density_kernel, n), out_shape=jax.ShapeD...  232 us
    transpose x1, local copies, waits for them, and re-layouts, fused_density(): jnp.transpose(phased, (2, 0, 1, 3)).reshape(n, each_b, 2, rows_c, width)  8.08 us

profile of v1, /device:TPU:0, one launch (start us, length us, event | category | flops | bytes accessed | tf_op | source)
XLA Modules:
  0.0 257.9 jit_solution(15861491607636944901)
XLA Ops:
  0.0 0.7 and_convert_fusion.4
  0.7 0.7 convert_multiply_fusion
  1.3 0.6 fusion.2
  1.9 1.3 add_multiply_fusion
  3.3 1.3 add_multiply_fusion.2
  4.6 0.7 and_convert_fusion.1
  5.3 1.1 sine_multiply_fusion
  6.4 1.3 add_multiply_fusion.1
  7.7 0.7 and_convert_fusion.3
  8.3 0.1 sine_multiply_fusion.1
  8.5 4.4 %multiply_add_fusion = (f32[1,16,128,512]{3,2,1,0:T(8,128)S(1)}, f32[1,16,128,512]{3,2,1,0:T(8,128)S(1)}) fusion(f32[2,16,128,512]{3,2,1,0:T(8,128)} %param.6, f32[16,128]{1,0:T(8,128)S(1)} %get-tuple-element.12, f32[128,512]{1,0:T(8,128)S(1)} %get-tuple-element.11, f32[16,128]{1,0:T(8,128)S(1)} %get-tuple-element.10, f32[128,512]{1,0:T(8,128)S(1)} %get-tuple-element.9), kind=kLoop, calls=%fused_computation.6 | loop fusion | flops 12582912 | bytes 17317888 | tf_op jit(solution)/shard_map/add | solution.py:60
  12.9 1.6 maximum_bitcast_fusion
  14.5 0.0 copy-start
  14.5 8.1 %copy.7 = f32[128,2,16,512]{3,2,1,0:T(8,128)} copy(f32[128,2,16,512]{3,0,2,1:T(8,128)S(1)} %maximum_bitcast_fusion) | data formatting | bytes 16777216 | tf_op jit(solution)/shard_map/transpose | solution.py:231
  22.6 0.0 copy-done
  22.6 0.2 slice_bitcast_fusion
  22.8 0.1 fusion.1
  22.9 2.2 fusion
  25.1 232.1 %shard_map.64 = f32[2,16,512]{2,1,0:T(8,128)S(1)} custom-call(f32[32,4,2,16,512]{4,3,2,1,0:T(8,128)} %bitcast.14, bf16[1024,1024]{1,0:T(8,128)(2,1)S(1)} %get-tuple-element.16.ah_ref, bf16[1024,1024]{1,0:T(8,128)(2,1)} %get-tuple-element.15.al_ref), custom_call_target="tpu_custom_call" | custom-call | tf_op jit(solution)/shard_map/pallas_call | solution.py:243
  257.2 0.7 copy.8
Async XLA Ops:
  14.5 8.1 %copy-start = (f32[2,512,512]{2,1,0:T(8,128)S(1)}, f32[2,512,512]{2,1,0:T(8,128)}, u32[]{:S(2)}) copy-start(f32[2,512,512]{2,1,0:T(8,128)} %param.7) | copy-start | bytes 6291460

commit v2 on v1

--- a/solution.py
+++ b/solution.py
@@ -75,17 +75,31 @@
     return one(left[0], right[0]) + (one(left[0], right[1]) + one(left[1], right[0]))
 
 
+def column(row):
+    size = row.shape[1]
+    at = lax.broadcasted_iota(jnp.int32, (size, size), 0)
+    across = lax.broadcasted_iota(jnp.int32, (size, size), 1)
+    picked = jnp.where(at == across, row.astype(jnp.float32), 0.0)
+    return jnp.sum(picked, axis=1, keepdims=True)
+
+
 def density_kernel(
-    n, x_ref, ah_ref, al_ref, out_ref,
+    n, amp_hbm, prop_hbm, first_ref, second_ref, third_ref, detune_ref, out_ref,
+    amp, prop, second_col, cos_ba, sin_ba, cos_cb, sin_cb, outgoing, ah_ref, al_ref,
     recv, xh, xl, vh, vl, total, kept, landing,
-    send_sem, recv_sem, half_send, half_recv,
+    load_sem, send_sem, recv_sem, half_send, half_recv,
 ):
     steps = half_send.shape[0]
     me = lax.axis_index("cfg")
-    each_b, rows_c = x_ref.shape[1], x_ref.shape[3]
-    width = x_ref.shape[4]
+    total_b, _, rows_c, width = outgoing.shape
+    each_b = total_b // n
     height = recv.shape[2]
     rows = out_ref.shape[1]
+
+    load_amp = pltpu.make_async_copy(amp_hbm, amp, load_sem.at[0])
+    load_prop = pltpu.make_async_copy(prop_hbm, prop, load_sem.at[1])
+    load_amp.start()
+    load_prop.start()
 
     barrier = pltpu.get_barrier_semaphore()
 
@@ -96,35 +110,117 @@
         return carry
 
     lax.fori_loop(1, n, greet, 0)
-    pl.semaphore_wait(barrier, n - 1)
-
-    def place(b):
-        return recv.at[b, :, pl.ds(pl.multiple_of(me * rows_c, rows_c), rows_c), :]
-
-    def send(b, s):
-        peer = lax.rem(me + s, n)
+
+    def scaled(which):
+        return detune_ref[which].astype(jnp.float32) * angle_step
+
+    first, second = first_ref[...], second_ref[...]
+    third = column(third_ref[...]).astype(jnp.int32)
+    near, last = atom_bit(second, 12), atom_bit(second, 13)
+    angle_cb = scaled(2) * occupation(third) + pair_angle * (
+        near * atom_bit(third, 0) + last * atom_bit(third, 1)
+    )
+    allowed_cb = 1.0 - last * atom_bit(third, 0)
+    cos_cb[...] = allowed_cb * jnp.cos(angle_cb)
+    sin_cb[...] = allowed_cb * jnp.sin(angle_cb)
+    second_col[...] = jnp.broadcast_to(column(second), second_col.shape)
+    phase_first = scaled(0) * occupation(first)
+    near_first, last_first = atom_bit(first, 12), atom_bit(first, 13)
+    step_second = scaled(1)
+
+    def table_rows(i, carry):
+        at = pl.ds(pl.multiple_of(i * 8, 8), 8)
+        mask = second_col[at, :][:, :1].astype(jnp.int32)
+        head, following = atom_bit(mask, 0), atom_bit(mask, 1)
+        angle = (
+            step_second * occupation(mask)
+            + phase_first
+            + pair_angle * (near_first * head + last_first * following)
+        )
+        allowed = 1.0 - last_first * head
+        cosine, sine = allowed * jnp.cos(angle), allowed * jnp.sin(angle)
+        for k in range(width // 128):
+            cos_ba[k, at, :] = cosine[:, k * 128 : (k + 1) * 128]
+            sin_ba[k, at, :] = sine[:, k * 128 : (k + 1) * 128]
+        return carry
+
+    lax.fori_loop(0, total_b // 8, table_rows, 0)
+
+    lane = lax.broadcasted_iota(jnp.int32, (rows_c, total_b), 1)
+    columns = width // 128
+    stride = total_b * columns
+
+    def produce(b):
+        here = lane == b
+        cos_c = jnp.sum(jnp.where(here, cos_cb[...], 0.0), axis=1, keepdims=True)
+        sin_c = jnp.sum(jnp.where(here, sin_cb[...], 0.0), axis=1, keepdims=True)
+        for k in range(columns):
+            lanes = slice(k * 128, (k + 1) * 128)
+            start = ((b // 8) * columns + k) * 8 + lax.rem(b, 8)
+            real = amp[0, pl.ds(start, rows_c, stride=stride), :]
+            imag = amp[1, pl.ds(start, rows_c, stride=stride), :]
+            cos_b = cos_ba[k, pl.ds(b, 1), :]
+            sin_b = sin_ba[k, pl.ds(b, 1), :]
+            cosine = cos_b * cos_c - sin_b * sin_c
+            sine = sin_b * cos_c + cos_b * sin_c
+            outgoing[b, 0, :, lanes] = real * cosine + imag * sine
+            outgoing[b, 1, :, lanes] = imag * cosine - real * sine
+
+    def place(j):
+        return recv.at[j, :, pl.ds(pl.multiple_of(me * rows_c, rows_c), rows_c), :]
+
+    def partner(i):
+        return lax.rem(me + n // 2 + ((i + 1) // 2) * (1 - 2 * lax.rem(i, 2)), n)
+
+    def send(i, j):
+        peer = partner(i)
         pltpu.make_async_remote_copy(
-            src_ref=x_ref.at[peer, b],
-            dst_ref=place(b),
-            send_sem=send_sem.at[b],
-            recv_sem=recv_sem.at[b],
+            src_ref=outgoing.at[peer * each_b + j],
+            dst_ref=place(j),
+            send_sem=send_sem.at[j],
+            recv_sem=recv_sem.at[j],
             device_id={"cfg": peer},
             device_id_type=MESH,
         ).start()
 
-    def send_all(b, carry):
-        pltpu.make_async_copy(x_ref.at[me, b], place(b), recv_sem.at[b]).start()
-
-        def pair(s, inner):
-            send(b, n // 2 + s)
-            send(b, n // 2 - s)
+    load_amp.wait()
+    pl.semaphore_wait(barrier, n - 1)
+
+    def send_all(j, carry):
+        produce(me * each_b + j)
+        produce(partner(0) * each_b + j)
+
+        def next_pair(i, inner):
+            produce(partner(i) * each_b + j)
+            send(i - 1, j)
             return inner
 
-        send(b, n // 2)
-        lax.fori_loop(1, n // 2, pair, 0)
+        lax.fori_loop(1, n - 1, next_pair, 0)
+        pltpu.make_async_copy(
+            outgoing.at[me * each_b + j], place(j), recv_sem.at[j]
+        ).start()
+        send(n - 2, j)
         return carry
 
     lax.fori_loop(0, each_b, send_all, 0)
+    load_prop.wait()
+
+    def split_prop(i, carry):
+        at = pl.ds(pl.multiple_of(i * 64, 64), 64)
+        below = pl.ds(pl.multiple_of(height + i * 64, 64), 64)
+        high, low = split(prop[0, at, :])
+        ah_ref[at, :height] = high
+        al_ref[at, :height] = low
+        ah_ref[below, height:] = high
+        al_ref[below, height:] = low
+        high, low = split(prop[1, at, :])
+        ah_ref[at, height:] = -high
+        al_ref[at, height:] = -low
+        ah_ref[below, :height] = high
+        al_ref[below, :height] = low
+        return carry
+
+    lax.fori_loop(0, height // 64, split_prop, 0)
     total[...] = jnp.zeros_like(total)
 
     tile = 256
@@ -216,36 +312,38 @@
         lax.fori_loop(0, half, add_next, 0)
     out_ref[...] = kept[:, offset]
 
-    for b in range(each_b):
+    for j in range(each_b):
         pltpu.make_async_copy(
-            x_ref.at[pl.ds(0, n - 1), b], x_ref.at[pl.ds(0, n - 1), b], send_sem.at[b]
+            outgoing.at[pl.ds(0, n - 1)], outgoing.at[pl.ds(0, n - 1)], send_sem.at[j]
         ).wait()
 
 
-def fused_density(phased, prop, n):
-    _, rows_c, total_b, width = phased.shape
+def fused_density(amplitudes, prop, first, second, third, detune_steps, n):
+    _, rows_c, total_b, width = amplitudes.shape
     height = prop.shape[1]
     each_b = total_b // n
     rows = width // n
     steps = n.bit_length() - 1
-    outgoing = jnp.transpose(phased, (2, 0, 1, 3)).reshape(n, each_b, 2, rows_c, width)
-    joined = jnp.concatenate(
-        [
-            jnp.concatenate([prop[0], -prop[1]], axis=1),
-            jnp.concatenate([prop[1], prop[0]], axis=1),
-        ],
-        axis=0,
-    )
-    high = lax.reduce_precision(joined, 8, 7)
-    low = (joined - high).astype(jnp.bfloat16)
-    high = high.astype(jnp.bfloat16)
+    tiled = amplitudes.reshape(2, rows_c, total_b // 8, 8, width // 128, 128)
+    tiled = jnp.transpose(tiled, (0, 1, 2, 4, 3, 5)).reshape(2, -1, 128)
     vmem = pl.BlockSpec(memory_space=pltpu.VMEM)
+    anywhere = pl.BlockSpec(memory_space=pl.ANY)
     result = pl.pallas_call(
         functools.partial(density_kernel, n),
         out_shape=jax.ShapeDtypeStruct((2, rows, width), jnp.float32),
-        in_specs=[pl.BlockSpec(memory_space=pl.ANY), vmem, vmem],
+        in_specs=[anywhere, anywhere, vmem, vmem, vmem, pl.BlockSpec(memory_space=pltpu.SMEM)],
         out_specs=vmem,
         scratch_shapes=[
+            pltpu.VMEM(tiled.shape, jnp.float32),
+            pltpu.VMEM(prop.shape, jnp.float32),
+            pltpu.VMEM((total_b, 128), jnp.float32),
+            pltpu.VMEM((width // 128, total_b, 128), jnp.float32),
+            pltpu.VMEM((width // 128, total_b, 128), jnp.float32),
+            pltpu.VMEM((rows_c, total_b), jnp.float32),
+            pltpu.VMEM((rows_c, total_b), jnp.float32),
+            pltpu.VMEM((total_b, 2, rows_c, width), jnp.float32),
+            pltpu.VMEM((2 * height, 2 * height), jnp.bfloat16),
+            pltpu.VMEM((2 * height, 2 * height), jnp.bfloat16),
             pltpu.VMEM((each_b, 2, height, width), jnp.float32),
             pltpu.VMEM((2 * height, width), jnp.bfloat16),
             pltpu.VMEM((2 * height, width), jnp.bfloat16),
@@ -254,15 +352,18 @@
             pltpu.VMEM((2, n // 2, 2, rows, width), jnp.float32),
             pltpu.VMEM((2, n // 2, rows, width), jnp.float32),
             pltpu.VMEM((2, n - 1, rows, width), jnp.float32),
+            pltpu.SemaphoreType.DMA((2,)),
             pltpu.SemaphoreType.DMA((each_b,)),
             pltpu.SemaphoreType.DMA((each_b,)),
             pltpu.SemaphoreType.DMA((steps,)),
             pltpu.SemaphoreType.DMA((steps,)),
         ],
         compiler_params=pltpu.CompilerParams(
-            collective_id=0, has_side_effects=True, vmem_limit_bytes=50 * 2**20
+            collective_id=0, has_side_effects=True, vmem_limit_bytes=56 * 2**20
         ),
-    )(outgoing, high, low)
+    )(
+        tiled, prop, first.reshape(1, -1), second.reshape(1, -1), third.reshape(1, -1), detune_steps
+    )
     return jnp.transpose(result, (1, 0, 2))
 
 
@@ -290,22 +391,25 @@
 
 
 def shards(n, amplitudes, prop_third, first, second, third, detune_steps):
-    phased = apply_phases(amplitudes, factor_tables(first, second, third, detune_steps))
-    _, rows_c, total_b, width = phased.shape
+    _, rows_c, total_b, width = amplitudes.shape
     height = prop_third.shape[1]
     fits = (
         n > 1
         and n & (n - 1) == 0
         and total_b % n == 0
+        and total_b % 128 == 0
         and rows_c % 8 == 0
         and width % (8 * n) == 0
         and width % 256 == 0
         and height % 256 == 0
         and 256 % (2 * (width // n)) == 0
-        and 4 * total_b // n * height * width * 2 <= 2**24
+        and 12 * rows_c * total_b * width <= 2**24
     )
     if fits:
-        return fused_density(phased, prop_third, n)
+        return fused_density(
+            amplitudes, prop_third, first, second, third, detune_steps, n
+        )
+    phased = apply_phases(amplitudes, factor_tables(first, second, third, detune_steps))
     return plain_density(phased, prop_third)
 
 

time: 258 us -> 233 us (0.903)
  other arithmetic: 16.2 us -> 0 us
  local copies, waits for them, and re-layouts: 9.55 us -> 1.52 us
    transpose x1 -> x0, local copies, waits for them, and re-layouts: 8.08 us -> none  [fused_density(): jnp.transpose(phased, (2, 0, 1, 3)).reshape(n, each_b, 2, rows_c, width)]
    mul x6 -> x0, other arithmetic: 5.83 us -> none  [the longest x1 1.33 us: factor_tables(): phase_first = scaled[0] * occupation(first)]
    add x1 -> x0, other arithmetic: 4.44 us -> none  [apply_phases(): amplitudes[0] * cosine + amplitudes[1] * sine]
    convert_element_type x4 -> x0, other arithmetic: 4.25 us -> none  [the longest x1 2.25 us: fused_density(): low = (joined - high).astype(jnp.bfloat16)]
where the time goes in v2:
time: 233 us
  Pallas kernels  231 us (99%)
    pallas_call x1, Pallas kernels, fused_density(): pl.pallas_call(functools.partial(density_kernel, n), out_shape=jax.ShapeD...  231 us

profile of v2, /device:TPU:0, one launch (start us, length us, event | category | flops | bytes accessed | tf_op | source)
XLA Modules:
  0.0 233.0 jit_solution(4886076428889925958)
XLA Ops:
  0.0 231.4 %shard_map.64 = f32[2,16,512]{2,1,0:T(8,128)} custom-call(f32[2,8192,128]{2,1,0:T(8,128)} %bitcast.9, f32[2,512,512]{2,1,0:T(8,128)} %prop_hbm.1, s32[1,512]{1,0:T(1,128)} %bitcast.11, s32[1,128]{1,0:T(1,128)} %bitcast.12, s32[1,16]{1,0:T(1,128)} %bitcast.13, s32[3]{0:T(128)} %detune_ref.1), custom_call_target="tpu_custom_call" | custom-call | tf_op jit(solution)/shard_map/pallas_call | solution.py:331
  231.4 1.5 copy.7

commit v3 on v2

--- a/solution.py
+++ b/solution.py
@@ -83,13 +83,21 @@
     return jnp.sum(picked, axis=1, keepdims=True)
 
 
+def part_order(part, steps):
+    order = list(range(steps))
+    if steps > 4:
+        turned = [(1, 2, 3), (2, 1, 3), (3, 1, 2), (3, 2, 1)][part % 4]
+        order[1:4] = turned
+    return order
+
+
 def density_kernel(
     n, amp_hbm, prop_hbm, first_ref, second_ref, third_ref, detune_ref, out_ref,
     amp, prop, second_col, cos_ba, sin_ba, cos_cb, sin_cb, outgoing, ah_ref, al_ref,
     recv, xh, xl, vh, vl, total, kept, landing,
     load_sem, send_sem, recv_sem, half_send, half_recv,
 ):
-    steps = half_send.shape[0]
+    steps = half_send.shape[1]
     me = lax.axis_index("cfg")
     total_b, _, rows_c, width = outgoing.shape
     each_b = total_b // n
@@ -269,48 +277,63 @@
 
     lax.fori_loop(0, each_b, work, 0)
 
-    def halve(step, src, half):
-        other = me + (1 - 2 * lax.rem(me // (2 ** step), 2)) * (2 ** step)
+    parts = width // 128
+    orders = [part_order(p, steps) for p in range(parts)]
+    offsets = [0] * parts
+
+    def bit_of(index, which):
+        return lax.rem(index // (2 ** which), 2)
+
+    def halve(p, t):
+        half = n >> (t + 1)
+        which = orders[p][t]
+        bit = bit_of(me, which)
+        lanes = pl.ds(p * 128, 128)
+        if t == 0:
+            src = total.at[:, :, 1 - bit, :, lanes]
+        else:
+            src = kept.at[:, pl.ds(offsets[p] + (1 - bit) * half, half), :, lanes]
+            offsets[p] = offsets[p] + bit * half
         copy = pltpu.make_async_remote_copy(
             src_ref=src,
-            dst_ref=landing.at[:, pl.ds(n - 2 * half, half)],
-            send_sem=half_send.at[step],
-            recv_sem=half_recv.at[step],
-            device_id={"cfg": other},
+            dst_ref=landing.at[:, pl.ds(n - 2 * half, half), :, lanes],
+            send_sem=half_send.at[p, t],
+            recv_sem=half_recv.at[p, t],
+            device_id={"cfg": me + (1 - 2 * bit) * (2 ** which)},
             device_id_type=MESH,
         )
         copy.start()
         return copy
 
-    half = n // 2
-    bit = lax.rem(me, 2)
-    copy = halve(0, total.at[:, :, 1 - bit], half)
-    copy.wait()
-
-    def add_first(i, carry):
-        where = 0
-        rest = i
-        for _ in range(steps - 1):
-            where = where * 2 + lax.rem(rest, 2)
-            rest = rest // 2
-        kept[:, where] = total[:, i, bit] + landing[:, i]
-        return carry
-
-    lax.fori_loop(0, half, add_first, 0)
-    offset = 0
-    for step in range(1, steps):
-        half = half // 2
-        bit = lax.rem(me // (2 ** step), 2)
-        copy = halve(step, kept.at[:, pl.ds(offset + (1 - bit) * half, half)], half)
-        offset = offset + bit * half
-        copy.wait()
-
-        def add_next(i, carry, offset=offset, half=half):
-            kept[:, offset + i] += landing[:, n - 2 * half + i]
-            return carry
-
-        lax.fori_loop(0, half, add_next, 0)
-    out_ref[...] = kept[:, offset]
+    def add(p, t):
+        half = n >> (t + 1)
+        lanes = slice(p * 128, (p + 1) * 128)
+        if t == 0:
+            core = bit_of(me, 0)
+
+            def add_first(i, carry):
+                where = 0
+                for which in orders[p][1:]:
+                    where = where * 2 + bit_of(i, which - 1)
+                kept[:, where, :, lanes] = total[:, i, core, :, lanes] + landing[:, i, :, lanes]
+                return carry
+
+            lax.fori_loop(0, half, add_first, 0)
+        else:
+            first = n - 2 * half
+            at = pl.ds(offsets[p], half)
+            kept[:, at, :, lanes] += landing[:, first : first + half, :, lanes]
+
+    flying = [halve(p, 0) for p in range(parts)]
+    for t in range(steps):
+        for p in range(parts):
+            flying[p].wait()
+            add(p, t)
+            if t + 1 < steps:
+                flying[p] = halve(p, t + 1)
+            else:
+                lanes = slice(p * 128, (p + 1) * 128)
+                out_ref[:, :, lanes] = kept[:, offsets[p], :, lanes]
 
     for j in range(each_b):
         pltpu.make_async_copy(
@@ -355,8 +378,8 @@
             pltpu.SemaphoreType.DMA((2,)),
             pltpu.SemaphoreType.DMA((each_b,)),
             pltpu.SemaphoreType.DMA((each_b,)),
-            pltpu.SemaphoreType.DMA((steps,)),
-            pltpu.SemaphoreType.DMA((steps,)),
+            pltpu.SemaphoreType.DMA((width // 128, steps)),
+            pltpu.SemaphoreType.DMA((width // 128, steps)),
         ],
         compiler_params=pltpu.CompilerParams(
             collective_id=0, has_side_effects=True, vmem_limit_bytes=56 * 2**20

time: 233 us -> 221 us (0.948)
  Pallas kernels: 231 us -> 219 us
    pallas_call x1, Pallas kernels: 231 us -> 219 us  [fused_density(): pl.pallas_call(functools.partial(density_kernel, n), out_shape=jax.ShapeD...]
where the time goes in v3:
time: 221 us
  Pallas kernels  219 us (99%)
    pallas_call x1, Pallas kernels, fused_density(): pl.pallas_call(functools.partial(density_kernel, n), out_shape=jax.ShapeD...  219 us

profile of v3, /device:TPU:0, one launch (start us, length us, event | category | flops | bytes accessed | tf_op | source)
XLA Modules:
  0.0 221.0 jit_solution(18305643091581794146)
XLA Ops:
  0.0 219.4 %shard_map.64 = f32[2,16,512]{2,1,0:T(8,128)} custom-call(f32[2,8192,128]{2,1,0:T(8,128)} %bitcast.9, f32[2,512,512]{2,1,0:T(8,128)} %prop_hbm.1, s32[1,512]{1,0:T(1,128)} %bitcast.11, s32[1,128]{1,0:T(1,128)} %bitcast.12, s32[1,16]{1,0:T(1,128)} %bitcast.13, s32[3]{0:T(128)} %detune_ref.1), custom_call_target="tpu_custom_call" | custom-call | tf_op jit(solution)/shard_map/pallas_call | solution.py:354
  219.4 1.5 copy.7

commit v4 on v3

--- a/solution.py
+++ b/solution.py
@@ -174,43 +174,61 @@
             outgoing[b, 0, :, lanes] = real * cosine + imag * sine
             outgoing[b, 1, :, lanes] = imag * cosine - real * sine
 
-    def place(j):
-        return recv.at[j, :, pl.ds(pl.multiple_of(me * rows_c, rows_c), rows_c), :]
+    def place(j, lanes):
+        return recv.at[j, :, pl.ds(pl.multiple_of(me * rows_c, rows_c), rows_c), lanes]
 
     def partner(i):
         return lax.rem(me + n // 2 + ((i + 1) // 2) * (1 - 2 * lax.rem(i, 2)), n)
 
-    def send(i, j):
+    def send(i, j, lanes, sem):
         peer = partner(i)
         pltpu.make_async_remote_copy(
-            src_ref=outgoing.at[peer * each_b + j],
-            dst_ref=place(j),
-            send_sem=send_sem.at[j],
-            recv_sem=recv_sem.at[j],
+            src_ref=outgoing.at[peer * each_b + j, :, :, lanes],
+            dst_ref=place(j, lanes),
+            send_sem=send_sem.at[sem],
+            recv_sem=recv_sem.at[sem],
             device_id={"cfg": peer},
             device_id_type=MESH,
         ).start()
 
+    def keep(j, lanes, sem):
+        pltpu.make_async_copy(
+            outgoing.at[me * each_b + j, :, :, lanes], place(j, lanes), recv_sem.at[sem]
+        ).start()
+
+    everything = pl.ds(0, width)
+    near_half, far_half = pl.ds(0, width // 2), pl.ds(width // 2, width // 2)
+
     load_amp.wait()
     pl.semaphore_wait(barrier, n - 1)
 
-    def send_all(j, carry):
+    def produce_all(j, lanes, sem):
         produce(me * each_b + j)
         produce(partner(0) * each_b + j)
 
         def next_pair(i, inner):
             produce(partner(i) * each_b + j)
-            send(i - 1, j)
+            send(i - 1, j, lanes, sem)
             return inner
 
         lax.fori_loop(1, n - 1, next_pair, 0)
-        pltpu.make_async_copy(
-            outgoing.at[me * each_b + j], place(j), recv_sem.at[j]
-        ).start()
-        send(n - 2, j)
-        return carry
-
-    lax.fori_loop(0, each_b, send_all, 0)
+        keep(j, lanes, sem)
+        send(n - 2, j, lanes, sem)
+
+    def send_all(j, carry):
+        produce_all(j, everything, j)
+        return carry
+
+    final = each_b - 1
+    lax.fori_loop(0, final, send_all, 0)
+    produce_all(final, near_half, final)
+
+    def send_rest(i, carry):
+        send(i, final, far_half, final + 1)
+        return carry
+
+    lax.fori_loop(0, n - 1, send_rest, 0)
+    keep(final, far_half, final + 1)
     load_prop.wait()
 
     def split_prop(i, carry):
@@ -231,19 +249,21 @@
     lax.fori_loop(0, height // 64, split_prop, 0)
     total[...] = jnp.zeros_like(total)
 
+    def arrived(b, lanes, sem):
+        pltpu.make_async_copy(
+            recv.at[b, :, :, lanes], recv.at[b, :, :, lanes], recv_sem.at[sem]
+        ).wait()
+
     tile = 256
-    pairs_per_tile = tile // (2 * rows)
-
-    def work(b, carry):
-        pltpu.make_async_copy(recv.at[b], recv.at[b], recv_sem.at[b]).wait()
-
+
+    def propagate(b, lanes):
         for part in range(2):
             def split_rows(t, inner):
                 at = pl.ds(pl.multiple_of(t * 64, 64), 64)
                 to = pl.ds(pl.multiple_of(part * height + t * 64, 64), 64)
-                high, low = split(recv[b, part, at, :])
-                xh[to, :] = high
-                xl[to, :] = low
+                high, low = split(recv[b, part, at, lanes])
+                xh[to, lanes] = high
+                xl[to, lanes] = low
                 return inner
 
             lax.fori_loop(0, height // 64, split_rows, 0)
@@ -251,31 +271,48 @@
         def evolve(t, inner):
             at = pl.ds(pl.multiple_of(t * tile, tile), tile)
             value = dot3(
-                (ah_ref[at, :], al_ref[at, :]), (xh[...], xl[...]), ((1,), (0,))
+                (ah_ref[at, :], al_ref[at, :]), (xh[:, lanes], xl[:, lanes]), ((1,), (0,))
             )
             high, low = split(value)
-            vh[at, :] = high
-            vl[at, :] = low
+            vh[at, lanes] = high
+            vl[at, lanes] = low
             return inner
 
         lax.fori_loop(0, 2 * height // tile, evolve, 0)
 
-        for t in range(width // tile):
-            at = slice(t * tile, (t + 1) * tile)
-            real = (vh[:height, :], vl[:height, :])
-            imag = (vh[height:, :], vl[height:, :])
-            real_t = (vh[:height, at], vl[:height, at])
-            imag_t = (vh[height:, at], vl[height:, at])
-            dims = ((0,), (0,))
+    def accumulate(left, right):
+        def pieces(lanes):
+            return (
+                (vh[:height, lanes], vl[:height, lanes]),
+                (vh[height:, lanes], vl[height:, lanes]),
+            )
+
+        real, imag = pieces(right)
+        dims = ((0,), (0,))
+        for at in range(left.start, left.stop, tile):
+            real_t, imag_t = pieces(slice(at, at + tile))
+            to = slice(at // (2 * rows), (at + tile) // (2 * rows))
+            shape = (tile // (2 * rows), 2, rows, right.stop - right.start)
             term_real = dot3(real_t, real, dims) + dot3(imag_t, imag, dims)
-            to = slice(t * pairs_per_tile, (t + 1) * pairs_per_tile)
-            shape = (pairs_per_tile, 2, rows, width)
-            total[0, to] += term_real.reshape(shape)
+            total[0, to, :, :, right] += term_real.reshape(shape)
             term_imag = dot3(imag_t, real, dims) - dot3(real_t, imag, dims)
-            total[1, to] += term_imag.reshape(shape)
-        return carry
-
-    lax.fori_loop(0, each_b, work, 0)
+            total[1, to, :, :, right] += term_imag.reshape(shape)
+
+    middle = width // 2
+    full, low_half, high_half = slice(0, width), slice(0, middle), slice(middle, width)
+
+    def work(b, carry):
+        arrived(b, everything, b)
+        propagate(b, full)
+        accumulate(full, full)
+        return carry
+
+    lax.fori_loop(0, final, work, 0)
+    arrived(final, near_half, final)
+    propagate(final, low_half)
+    accumulate(low_half, low_half)
+    arrived(final, far_half, final + 1)
+    propagate(final, high_half)
 
     parts = width // 128
     orders = [part_order(p, steps) for p in range(parts)]
@@ -324,9 +361,15 @@
             at = pl.ds(offsets[p], half)
             kept[:, at, :, lanes] += landing[:, first : first + half, :, lanes]
 
-    flying = [halve(p, 0) for p in range(parts)]
+    flying = {}
+    accumulate(full, high_half)
+    for p in range(parts // 2, parts):
+        flying[p] = halve(p, 0)
+    accumulate(high_half, low_half)
+    for p in range(parts // 2):
+        flying[p] = halve(p, 0)
     for t in range(steps):
-        for p in range(parts):
+        for p in list(flying):
             flying[p].wait()
             add(p, t)
             if t + 1 < steps:
@@ -335,10 +378,9 @@
                 lanes = slice(p * 128, (p + 1) * 128)
                 out_ref[:, :, lanes] = kept[:, offsets[p], :, lanes]
 
-    for j in range(each_b):
-        pltpu.make_async_copy(
-            outgoing.at[pl.ds(0, n - 1)], outgoing.at[pl.ds(0, n - 1)], send_sem.at[j]
-        ).wait()
+    for j, lanes in enumerate([everything] * final + [near_half, far_half]):
+        sent = outgoing.at[pl.ds(0, n - 1), :, :, lanes]
+        pltpu.make_async_copy(sent, sent, send_sem.at[j]).wait()
 
 
 def fused_density(amplitudes, prop, first, second, third, detune_steps, n):
@@ -376,8 +418,8 @@
             pltpu.VMEM((2, n // 2, rows, width), jnp.float32),
             pltpu.VMEM((2, n - 1, rows, width), jnp.float32),
             pltpu.SemaphoreType.DMA((2,)),
-            pltpu.SemaphoreType.DMA((each_b,)),
-            pltpu.SemaphoreType.DMA((each_b,)),
+            pltpu.SemaphoreType.DMA((each_b + 1,)),
+            pltpu.SemaphoreType.DMA((each_b + 1,)),
             pltpu.SemaphoreType.DMA((width // 128, steps)),
             pltpu.SemaphoreType.DMA((width // 128, steps)),
         ],
@@ -423,7 +465,7 @@
         and total_b % 128 == 0
         and rows_c % 8 == 0
         and width % (8 * n) == 0
-        and width % 256 == 0
+        and width % 512 == 0
         and height % 256 == 0
         and 256 % (2 * (width // n)) == 0
         and 12 * rows_c * total_b * width <= 2**24

time: 221 us -> 218 us (0.986)
    pallas_call x1, Pallas kernels: 219 us -> 217 us  [fused_density(): pl.pallas_call(functools.partial(density_kernel, n), out_shape=jax.ShapeD...]
where the time goes in v4:
time: 218 us
  Pallas kernels  217 us (100%)
    pallas_call x1, Pallas kernels, fused_density(): pl.pallas_call(functools.partial(density_kernel, n), out_shape=jax.ShapeD...  217 us

profile of v4, /device:TPU:0, one launch (start us, length us, event | category | flops | bytes accessed | tf_op | source)
XLA Modules:
  0.0 218.1 jit_solution(8218460155491446049)
XLA Ops:
  0.0 216.6 %shard_map.64 = f32[2,16,512]{2,1,0:T(8,128)} custom-call(f32[2,8192,128]{2,1,0:T(8,128)} %bitcast.9, f32[2,512,512]{2,1,0:T(8,128)} %prop_hbm.1, s32[1,512]{1,0:T(1,128)} %bitcast.11, s32[1,128]{1,0:T(1,128)} %bitcast.12, s32[1,16]{1,0:T(1,128)} %bitcast.13, s32[3]{0:T(128)} %detune_ref.1), custom_call_target="tpu_custom_call" | custom-call | tf_op jit(solution)/shard_map/pallas_call | solution.py:396
  216.6 1.5 copy.7

commit v5 on v4

--- a/solution.py
+++ b/solution.py
@@ -178,7 +178,11 @@
         return recv.at[j, :, pl.ds(pl.multiple_of(me * rows_c, rows_c), rows_c), lanes]
 
     def partner(i):
-        return lax.rem(me + n // 2 + ((i + 1) // 2) * (1 - 2 * lax.rem(i, 2)), n)
+        k, odd = i // 2, lax.rem(i, 2)
+        turn = lax.rem(k, 2)
+        far = n // 2 + ((k + 1) // 2) * (1 - 2 * turn)
+        near = (1 - turn) * (n - 1 - k // 2) + turn * ((k + 1) // 2)
+        return lax.rem(me + (1 - odd) * far + odd * near, n)
 
     def send(i, j, lanes, sem):
         peer = partner(i)
@@ -204,7 +208,7 @@
 
     def produce_all(j, lanes, sem):
         produce(me * each_b + j)
-        produce(partner(0) * each_b + j)
+        produce(partner(jnp.int32(0)) * each_b + j)
 
         def next_pair(i, inner):
             produce(partner(i) * each_b + j)
@@ -213,7 +217,7 @@
 
         lax.fori_loop(1, n - 1, next_pair, 0)
         keep(j, lanes, sem)
-        send(n - 2, j, lanes, sem)
+        send(jnp.int32(n - 2), j, lanes, sem)
 
     def send_all(j, carry):
         produce_all(j, everything, j)

time: 218 us -> 217 us (level)
  no operation moved by 1% of the time
where the time goes in v5:
time: 217 us
  Pallas kernels  216 us (100%)
    pallas_call x1, Pallas kernels, fused_density(): pl.pallas_call(functools.partial(density_kernel, n), out_shape=jax.ShapeD...  216 us

profile of v5, /device:TPU:0, one launch (start us, length us, event | category | flops | bytes accessed | tf_op | source)
XLA Modules:
  0.0 217.2 jit_solution(1457412198756233999)
XLA Ops:
  0.0 215.6 %shard_map.64 = f32[2,16,512]{2,1,0:T(8,128)} custom-call(f32[2,8192,128]{2,1,0:T(8,128)} %bitcast.9, f32[2,512,512]{2,1,0:T(8,128)} %prop_hbm.1, s32[1,512]{1,0:T(1,128)} %bitcast.11, s32[1,128]{1,0:T(1,128)} %bitcast.12, s32[1,16]{1,0:T(1,128)} %bitcast.13, s32[3]{0:T(128)} %detune_ref.1), custom_call_target="tpu_custom_call" | custom-call | tf_op jit(solution)/shard_map/pallas_call | solution.py:400
  215.6 1.5 copy.7
